TPU v7x, 512 devices: a whole 4x8x8 slice. The times are simulated.
512 devices in a mesh: panel: 2 (over z_hi), colat: 16 (over z_lo, x), lon: 16 (over y, core).
Axes of the slice: x: 4, y: 8, z: 8 (z_hi: 2, z_lo: 4; z = z_hi * 4 + z_lo), core: 2. Of those that a mesh axis runs over, the one named last changes fastest.
Arguments:
- fields_now: float32 [4, 2, 256, 512, 128], P(None, 'panel', 'colat', 'lon'), may hold values from -6 to 6
- diffusivity: float32 [2, 256, 512, 128], P('panel', 'colat', 'lon'), may hold values from 0.5 to 2
- viscosity: float32 [2, 256, 512, 128], P('panel', 'colat', 'lon'), may hold values from 0.5 to 2
- donor_row: int32 [2, 16, 16, 12], P('panel', 'colat', 'lon'), may hold values from 0 to 16
- donor_column: int32 [2, 16, 16, 12], P('panel', 'colat', 'lon'), may hold values from 0 to 32
- donor_offset: float32 [2, 16, 16, 2, 12], P('panel', 'colat', 'lon'), may hold values from 0 to 1
- rim_angle: float32 [2, 16, 16, 12], P('panel', 'colat', 'lon'), may hold values from -3.140625 to 3.140625
Outputs:
- advanced: float32 [4, 2, 256, 512, 128], P(None, 'panel', 'colat', 'lon')
All inputs are finite; a program needn't handle non-finite values.
Results may differ from a plain program's by a relative error of at most 0.00002.
Values sent between devices are 32-bit elements; how exact they have to be, the bound alone decides.
A program may use at most 64 MiB of HBM per device.

v0:
```python
import jax
import jax.numpy as jnp
from jax import lax
from jax.sharding import PartitionSpec as P

TIME_STEP = 0.05
BUOYANCY = 1.0


def with_halo(x, sides, width):
    for axis, dim in sides:
        count, length = (lax.axis_size(axis), x.shape[dim])
        up = [(i, (i + 1) % count) for i in range(count - 1)]
        down = [(j, i) for i, j in up]
        last = lax.slice_in_dim(x, length - width, length, axis=dim)
        leading = lax.slice_in_dim(x, 0, width, axis=dim)
        before = lax.ppermute(last, axis, up)
        after = lax.ppermute(leading, axis, down)
        x = jnp.concatenate([before, x, after], axis=dim)
    return x


def swapped(block, axis, stride):
    count = lax.axis_size(axis)
    route = []
    for low in range(count):
        high = low | 1 << stride
        if high != low and high < count:
            route += [(low, high), (high, low)]
    return lax.ppermute(block, axis, route)


def gradient(stencil):
    return (8.0 * (stencil[3] - stencil[1]) - (stencil[4] - stencil[0])) / 12.0


def curvature(stencil):
    return (16.0 * (stencil[3] + stencil[1]) - (stencil[4] + stencil[0]) - 30.0 * stencil[2]) / 12.0


def advance(padded, thermal, viscous):
    height = padded.shape[1] - 4
    breadth = padded.shape[2] - 4
    center = padded[:, 2 : 2 + height, 2 : 2 + breadth]
    radial_len = center.shape[3]
    radial_pad = jnp.pad(center, ((0, 0), (0, 0), (0, 0), (2, 2)))
    along_lat = [padded[:, offset : offset + height, 2 : 2 + breadth] for offset in range(5)]
    along_lon = [padded[:, 2 : 2 + height, offset : offset + breadth] for offset in range(5)]
    along_rad = [radial_pad[..., offset : offset + radial_len] for offset in range(5)]
    laplace = curvature(along_rad) + curvature(along_lat) + curvature(along_lon)
    transport = (
        center[1:2] * gradient(along_rad)
        + center[2:3] * gradient(along_lat)
        + center[3:4] * gradient(along_lon)
    )
    diffusion = jnp.stack([thermal, viscous, viscous, viscous])
    change = diffusion * laplace - transport
    change = change.at[1].add(BUOYANCY * center[0])
    return center + TIME_STEP * change


def local(fields_now, diffusivity, viscosity, donor_row, donor_column, donor_offset, rim_angle):
    fields = fields_now[:, 0]
    thermal = diffusivity[0]
    viscous = viscosity[0]
    height = fields.shape[1]
    breadth = fields.shape[2]
    radial_len = fields.shape[3]
    colat_pos = lax.axis_index("colat")
    lon_pos = lax.axis_index("lon")
    colat_count = lax.axis_size("colat")
    lon_count = lax.axis_size("lon")
    row_share = 4 * breadth // colat_count
    padded = with_halo(fields, (("colat", 1), ("lon", 2)), 2)
    fresh = advance(padded, thermal, viscous)
    extended = with_halo(fresh, (("colat", 1), ("lon", 2)), 1)
    width = breadth + 2
    flattened = extended.reshape(4, (height + 2) * width, radial_len)
    anchor = donor_row.reshape(-1) * width + donor_column.reshape(-1)

    def corner(offset):
        return jnp.take(flattened, anchor + offset, axis=1)

    frac_row = donor_offset[0, 0, 0, 0][None, :, None]
    frac_lon = donor_offset[0, 0, 0, 1][None, :, None]
    blended = (1.0 - frac_row) * (
        (1.0 - frac_lon) * corner(0) + frac_lon * corner(1)
    ) + frac_row * ((1.0 - frac_lon) * corner(width) + frac_lon * corner(width + 1))
    angles = rim_angle.reshape(-1)
    cosine = jnp.cos(angles)[:, None]
    sine_part = jnp.sin(angles)[:, None]
    turned_lat = cosine * blended[2] - sine_part * blended[3]
    turned_lon = sine_part * blended[2] + cosine * blended[3]
    blended = jnp.stack([blended[0], blended[1], turned_lat, turned_lon])
    arrived = swapped(blended, "panel", 0)
    row_full = lax.all_gather(arrived[:, 0:row_share], "colat", axis=1, tiled=True)
    col_full = lax.all_gather(arrived[:, row_share:], "lon", axis=1, tiled=True)
    col_blocks = col_full.reshape(4, 4, height, radial_len)
    west_strip = jnp.transpose(
        jnp.stack([col_blocks[:, 0], col_blocks[:, 2]], axis=1), (0, 2, 1, 3)
    )
    east_strip = jnp.transpose(
        jnp.stack([col_blocks[:, 3], col_blocks[:, 1]], axis=1), (0, 2, 1, 3)
    )
    fresh = fresh.at[:, :, 0:2].set(jnp.where(lon_pos == 0, west_strip, fresh[:, :, 0:2]))
    fresh = fresh.at[:, :, breadth - 2 :].set(
        jnp.where(lon_pos == lon_count - 1, east_strip, fresh[:, :, breadth - 2 :])
    )
    row_blocks = row_full.reshape(4, 4, breadth, radial_len)
    north_strip = jnp.stack([row_blocks[:, 0], row_blocks[:, 2]], axis=1)
    south_strip = jnp.stack([row_blocks[:, 3], row_blocks[:, 1]], axis=1)
    fresh = fresh.at[:, 0:2].set(jnp.where(colat_pos == 0, north_strip, fresh[:, 0:2]))
    fresh = fresh.at[:, height - 2 :].set(
        jnp.where(colat_pos == colat_count - 1, south_strip, fresh[:, height - 2 :])
    )
    return fresh[:, None]


def solution(mesh):
    placed = (
        P(None, "panel", "colat", "lon", None),
        P("panel", "colat", "lon", None),
        P("panel", "colat", "lon", None),
        P("panel", "colat", "lon", None),
        P("panel", "colat", "lon", None),
        P("panel", "colat", "lon", None, None),
        P("panel", "colat", "lon", None),
    )
    return jax.shard_map(
        local,
        mesh=mesh,
        in_specs=placed,
        out_specs=P(None, "panel", "colat", "lon", None),
        check_vma=False,
    )
```

profile of v0, /device:TPU:24, one launch (start us, length us, event | category | flops | bytes accessed | tf_op | source)
XLA Modules:
  0.0 119.8 jit_solution(8745832736168921647)
XLA Ops:
  0.0 0.0 copy-start
  0.0 1.9 %copy.67 = f32[4,1,16,32,128]{4,2,3,0,1:T(8,128)S(1)} copy(f32[4,1,16,32,128]{4,3,2,1,0:T(8,128)} %param.19) | data formatting | bytes 2097152 | tf_op args[0]
  1.9 0.0 copy-start.3
  1.9 0.1 fusion.16
  2.0 1.3 %collective-permute-start = (f32[4,2,32,128]{3,1,2,0:T(2,128)S(1)}, f32[4,2,32,128]{3,1,2,0:T(2,128)S(1)}, u32[]{:S(2)}, u32[]{:S(2)}) collective-permute-start(f32[4,2,32,128]{3,1,2,0:T(2,128)S(1)} %get-tuple-element.87), channel_id=1, source_target_pairs={{16,0},{32,16},{48,32},{64,48},{80,64},{96,80},{112,96},{128,112},... | collective-permute-start | bytes 393224 | tf_op jit(solution)/shard_map/ppermute | solution.py:18
  3.3 0.0 copy-start.1
  3.4 0.0 copy-start.2
  3.4 4.7 %collective-permute-start.1 = (f32[4,2,32,128]{3,1,2,0:T(2,128)S(1)}, f32[4,2,32,128]{3,1,2,0:T(2,128)S(1)}, u32[]{:S(2)}, u32[]{:S(2)}) collective-permute-start(f32[4,2,32,128]{3,1,2,0:T(2,128)S(1)} %get-tuple-element.86), channel_id=1, source_target_pairs={{0,16},{16,32},{32,48},{48,64},{64,80},{80,96},{96,112},{112,128},... | collective-permute-start | bytes 393224 | tf_op jit(solution)/shard_map/ppermute | solution.py:17
  8.1 0.0 copy-done
  8.1 0.1 fusion.15
  8.2 0.0 copy-done.3
  8.2 0.0 copy-start.4
  8.2 0.0 copy-start.5
  8.2 0.0 copy-start.6
  8.3 0.2 copy.42
  8.4 0.2 copy.43
  8.6 0.2 copy.44
  8.8 0.0 copy-done.1
  8.8 0.2 copy.38
  8.9 0.0 copy-done.2
  9.0 0.2 copy.39
  9.1 0.0 copy-done.4
  9.1 0.0 copy-done.5
  9.2 0.0 copy-done.6
  9.2 0.0 collective-permute-done
  9.2 1.3 %collective-permute-done.1 = f32[4,2,32,128]{3,1,2,0:T(2,128)S(1)} collective-permute-done((f32[4,2,32,128]{3,1,2,0:T(2,128)S(1)}, f32[4,2,32,128]{3,1,2,0:T(2,128)S(1)}, u32[]{:S(2)}, u32[]{:S(2)}) %collective-permute-start.1) | collective-permute-done | bytes 131104 | tf_op jit(solution)/shard_map/ppermute | solution.py:17
  10.6 1.9 %collective-permute-start.2 = (f32[4,20,2,128]{3,1,2,0:T(8,128)S(1)}, f32[4,20,2,128]{3,1,2,0:T(8,128)S(1)}, u32[]{:S(2)}, u32[]{:S(2)}) collective-permute-start(f32[4,20,2,128]{3,1,2,0:T(8,128)S(1)} %get-tuple-element.76), channel_id=1, source_target_pairs={{1,0},{2,1},{3,2},{4,3},{5,4},{6,5},{7,6},{8,7},{9,8},{10,9},{11,1... | collective-permute-start | bytes 245768 | tf_op jit(solution)/shard_map/ppermute | solution.py:18
  12.5 2.4 %collective-permute-start.3 = (f32[4,20,2,128]{3,1,2,0:T(8,128)S(1)}, f32[4,20,2,128]{3,1,2,0:T(8,128)S(1)}, u32[]{:S(2)}, u32[]{:S(2)}) collective-permute-start(f32[4,20,2,128]{3,1,2,0:T(8,128)S(1)} %get-tuple-element.77), channel_id=1, source_target_pairs={{0,1},{1,2},{2,3},{3,4},{4,5},{5,6},{6,7},{7,8},{8,9},{9,10},{10,1... | collective-permute-start | bytes 245768 | tf_op jit(solution)/shard_map/ppermute | solution.py:17
  14.9 0.0 collective-permute-done.2
  15.0 3.5 %collective-permute-done.3 = f32[4,20,2,128]{3,1,2,0:T(8,128)S(1)} collective-permute-done((f32[4,20,2,128]{3,1,2,0:T(8,128)S(1)}, f32[4,20,2,128]{3,1,2,0:T(8,128)S(1)}, u32[]{:S(2)}, u32[]{:S(2)}) %collective-permute-start.3) | collective-permute-done | bytes 81952 | tf_op jit(solution)/shard_map/ppermute | solution.py:17
  18.5 0.3 pad_maximum_fusion
  18.7 2.5 %fusion.2 = f32[4,16,32,128]{3,1,2,0:T(8,128)S(1)} fusion(f32[1,16,32,128]{3,1,2,0:T(8,128)S(1)} %copy.39, f32[1,16,32,128]{3,1,2,0:T(8,128)S(1)} %copy.38, f32[4,20,34,128]{3,1,2,0:T(8,128)S(1)} %get-tuple-element.75, f32[4,20,34,128]{3,1,2,0:T(8,128)S(1)} %get-tuple-element.74, f32[4,2,32,128]{3,1,2,0:T(2,128)S(1)} %collective-permute-done, ...), kind=kLoop, calls=%fused_computation.20 | loop fusion | flops 11796480 | bytes 7864320 | tf_op jit(solution)/shard_map/sub | solution.py:57
  21.2 0.2 fusion.3
  21.5 0.7 multiply_add_fusion
  22.1 0.1 fusion.14
  22.2 4.4 %collective-permute-start.4 = (f32[4,1,32,128]{3,1,2,0:T(1,128)S(1)}, f32[4,1,32,128]{3,1,2,0:T(1,128)S(1)}, u32[]{:S(2)}, u32[]{:S(2)}) collective-permute-start(f32[4,1,32,128]{3,1,2,0:T(1,128)S(1)} %get-tuple-element.80), channel_id=1, source_target_pairs={{0,16},{16,32},{32,48},{48,64},{64,80},{80,96},{96,112},{112,128},... | collective-permute-start | bytes 196616 | tf_op jit(solution)/shard_map/ppermute | solution.py:17
  26.6 1.3 %collective-permute-start.5 = (f32[4,1,32,128]{3,1,2,0:T(1,128)S(1)}, f32[4,1,32,128]{3,1,2,0:T(1,128)S(1)}, u32[]{:S(2)}, u32[]{:S(2)}) collective-permute-start(f32[4,1,32,128]{3,1,2,0:T(1,128)S(1)} %get-tuple-element.81), channel_id=1, source_target_pairs={{16,0},{32,16},{48,32},{64,48},{80,64},{96,80},{112,96},{128,112},... | collective-permute-start | bytes 196616 | tf_op jit(solution)/shard_map/ppermute | solution.py:18
  27.9 0.7 collective-permute-done.4
  28.6 4.2 %collective-permute-done.5 = f32[4,1,32,128]{3,1,2,0:T(1,128)S(1)} collective-permute-done((f32[4,1,32,128]{3,1,2,0:T(1,128)S(1)}, f32[4,1,32,128]{3,1,2,0:T(1,128)S(1)}, u32[]{:S(2)}, u32[]{:S(2)}) %collective-permute-start.5) | collective-permute-done | bytes 65568 | tf_op jit(solution)/shard_map/ppermute | solution.py:18
  32.8 1.9 %collective-permute-start.6 = (f32[4,18,1,128]{3,1,2,0:T(8,128)S(1)}, f32[4,18,1,128]{3,1,2,0:T(8,128)S(1)}, u32[]{:S(2)}, u32[]{:S(2)}) collective-permute-start(f32[4,18,1,128]{3,1,2,0:T(8,128)S(1)} %get-tuple-element.78), channel_id=1, source_target_pairs={{0,1},{1,2},{2,3},{3,4},{4,5},{5,6},{6,7},{7,8},{8,9},{9,10},{10,1... | collective-permute-start | bytes 110600 | tf_op jit(solution)/shard_map/ppermute | solution.py:17
  34.7 3.6 %collective-permute-start.7 = (f32[4,18,1,128]{3,1,2,0:T(8,128)S(1)}, f32[4,18,1,128]{3,1,2,0:T(8,128)S(1)}, u32[]{:S(2)}, u32[]{:S(2)}) collective-permute-start(f32[4,18,1,128]{3,1,2,0:T(8,128)S(1)} %get-tuple-element.79), channel_id=1, source_target_pairs={{1,0},{2,1},{3,2},{4,3},{5,4},{6,5},{7,6},{8,7},{9,8},{10,9},{11,1... | collective-permute-start | bytes 110600 | tf_op jit(solution)/shard_map/ppermute | solution.py:18
  38.4 0.0 collective-permute-done.6
  38.4 3.1 %collective-permute-done.7 = f32[4,18,1,128]{3,1,2,0:T(8,128)S(1)} collective-permute-done((f32[4,18,1,128]{3,1,2,0:T(8,128)S(1)}, f32[4,18,1,128]{3,1,2,0:T(8,128)S(1)}, u32[]{:S(2)}, u32[]{:S(2)}) %collective-permute-start.7) | collective-permute-done | bytes 36896 | tf_op jit(solution)/shard_map/ppermute | solution.py:18
  41.4 0.3 pad_maximum_fusion.1
  41.7 0.5 copy.46
  42.2 0.6 gather_fusion.2
  42.8 0.6 gather_fusion.3
  43.4 0.6 gather_fusion.1
  43.9 0.6 gather_fusion
  44.5 0.2 fusion.11
  44.7 0.1 multiply_subtract_fusion
  44.8 10.9 %collective-permute-start.8 = (f32[4,12,128]{2,0,1:T(4,128)S(1)}, f32[4,12,128]{2,0,1:T(4,128)S(1)}, u32[]{:S(2)}, u32[]{:S(2)}) collective-permute-start(f32[4,12,128]{2,0,1:T(4,128)S(1)} %pad_maximum_fusion.10), channel_id=1, source_target_pairs={{0,256},{256,0},{1,257},{257,1},{2,258},{258,2},{3,259},{259,3},{4... | collective-permute-start | bytes 73736 | tf_op jit(solution)/shard_map/ppermute | solution.py:30
  55.8 1.8 %collective-permute-done.8 = f32[4,12,128]{2,0,1:T(4,128)S(1)} collective-permute-done((f32[4,12,128]{2,0,1:T(4,128)S(1)}, f32[4,12,128]{2,0,1:T(4,128)S(1)}, u32[]{:S(2)}, u32[]{:S(2)}) %collective-permute-start.8) | collective-permute-done | bytes 24608 | tf_op jit(solution)/shard_map/ppermute | solution.py:30
  57.6 17.1 %all_gather.6 = f32[4,64,128]{2,0,1:T(4,128)S(1)} all-gather(f32[4,4,128]{2,0,1:T(4,128)S(1)} %slice.349), channel_id=1, replica_groups=mesh['panel'=2,'colat'=16,'lon'=16] {'lon'}, dimensions={1}, use_global_device_ids=true | all-gather | bytes 139264 | tf_op jit(solution)/shard_map/all_gather | solution.py:97
  74.7 42.9 %all_gather.7 = f32[4,128,128]{2,0,1:T(4,128)S(1)} all-gather(f32[4,8,128]{2,0,1:T(4,128)S(1)} %slice.356), channel_id=1, replica_groups=mesh['panel'=2,'colat'=16,'lon'=16] {'colat'}, dimensions={1}, use_global_device_ids=true | all-gather | bytes 278528 | tf_op jit(solution)/shard_map/all_gather | solution.py:96
  117.6 0.1 copy.57
  117.7 0.1 copy.58
  117.8 0.2 fusion.6
  118.0 0.1 copy.72
  118.1 0.1 copy.59
  118.2 0.1 copy.60
  118.3 0.2 fusion.5
  118.5 1.3 %copy.53 = f32[4,1,16,32,128]{4,3,2,1,0:T(8,128)} copy(f32[4,1,16,32,128]{4,2,3,0,1:T(8,128)S(1)} %fusion.5) | data formatting | bytes 2097152 | tf_op jit(solution)/shard_map/scatter | solution.py:113
  (20 shorter events, 0.3 us)
Async XLA Ops:
  0.0 8.1 %copy-start = (f32[4,1,16,32,128]{4,3,2,1,0:T(8,128)S(1)}, f32[4,1,16,32,128]{4,3,2,1,0:T(8,128)}, u32[]{:S(2)}) copy-start(f32[4,1,16,32,128]{4,3,2,1,0:T(8,128)} %param.19) | copy-start | bytes 3145732
  1.9 6.3 %copy-start.3 = (f32[1,1,1,2,12]{4,3,2,1,0:T(2,128)S(1)}, f32[1,1,1,2,12]{4,3,2,1,0:T(2,128)}, u32[]{:S(2)}) copy-start(f32[1,1,1,2,12]{4,3,2,1,0:T(2,128)} %param.24) | copy-start | bytes 292
  2.0 7.2 %collective-permute-start = (f32[4,2,32,128]{3,1,2,0:T(2,128)S(1)}, f32[4,2,32,128]{3,1,2,0:T(2,128)S(1)}, u32[]{:S(2)}, u32[]{:S(2)}) collective-permute-start(f32[4,2,32,128]{3,1,2,0:T(2,128)S(1)} %get-tuple-element.87), channel_id=1, source_target_pairs={{16,0},{32,16},{48,32},{64,48},{80,64},{96,80},{112,96},{128,112},... | collective-permute-start | bytes 393224 | tf_op jit(solution)/shard_map/ppermute | solution.py:18
  3.3 5.4 %copy-start.1 = (f32[1,16,32,128]{3,2,1,0:T(8,128)S(1)}, f32[1,16,32,128]{3,2,1,0:T(8,128)}, u32[]{:S(2)}) copy-start(f32[1,16,32,128]{3,2,1,0:T(8,128)} %param.20) | copy-start | bytes 786436
  3.4 5.6 %copy-start.2 = (f32[1,16,32,128]{3,2,1,0:T(8,128)S(1)}, f32[1,16,32,128]{3,2,1,0:T(8,128)}, u32[]{:S(2)}) copy-start(f32[1,16,32,128]{3,2,1,0:T(8,128)} %param.21) | copy-start | bytes 786436
  3.4 7.2 %collective-permute-start.1 = (f32[4,2,32,128]{3,1,2,0:T(2,128)S(1)}, f32[4,2,32,128]{3,1,2,0:T(2,128)S(1)}, u32[]{:S(2)}, u32[]{:S(2)}) collective-permute-start(f32[4,2,32,128]{3,1,2,0:T(2,128)S(1)} %get-tuple-element.86), channel_id=1, source_target_pairs={{0,16},{16,32},{32,48},{48,64},{64,80},{80,96},{96,112},{112,128},... | collective-permute-start | bytes 393224 | tf_op jit(solution)/shard_map/ppermute | solution.py:17
  8.2 0.9 copy-start.4
  8.2 0.9 copy-start.5
  8.2 0.9 copy-start.6
  10.6 4.4 %collective-permute-start.2 = (f32[4,20,2,128]{3,1,2,0:T(8,128)S(1)}, f32[4,20,2,128]{3,1,2,0:T(8,128)S(1)}, u32[]{:S(2)}, u32[]{:S(2)}) collective-permute-start(f32[4,20,2,128]{3,1,2,0:T(8,128)S(1)} %get-tuple-element.76), channel_id=1, source_target_pairs={{1,0},{2,1},{3,2},{4,3},{5,4},{6,5},{7,6},{8,7},{9,8},{10,9},{11,1... | collective-permute-start | bytes 245768 | tf_op jit(solution)/shard_map/ppermute | solution.py:18
  12.5 5.9 %collective-permute-start.3 = (f32[4,20,2,128]{3,1,2,0:T(8,128)S(1)}, f32[4,20,2,128]{3,1,2,0:T(8,128)S(1)}, u32[]{:S(2)}, u32[]{:S(2)}) collective-permute-start(f32[4,20,2,128]{3,1,2,0:T(8,128)S(1)} %get-tuple-element.77), channel_id=1, source_target_pairs={{0,1},{1,2},{2,3},{3,4},{4,5},{5,6},{6,7},{7,8},{8,9},{9,10},{10,1... | collective-permute-start | bytes 245768 | tf_op jit(solution)/shard_map/ppermute | solution.py:17
  22.2 6.4 %collective-permute-start.4 = (f32[4,1,32,128]{3,1,2,0:T(1,128)S(1)}, f32[4,1,32,128]{3,1,2,0:T(1,128)S(1)}, u32[]{:S(2)}, u32[]{:S(2)}) collective-permute-start(f32[4,1,32,128]{3,1,2,0:T(1,128)S(1)} %get-tuple-element.80), channel_id=1, source_target_pairs={{0,16},{16,32},{32,48},{48,64},{64,80},{80,96},{96,112},{112,128},... | collective-permute-start | bytes 196616 | tf_op jit(solution)/shard_map/ppermute | solution.py:17
  26.6 6.2 %collective-permute-start.5 = (f32[4,1,32,128]{3,1,2,0:T(1,128)S(1)}, f32[4,1,32,128]{3,1,2,0:T(1,128)S(1)}, u32[]{:S(2)}, u32[]{:S(2)}) collective-permute-start(f32[4,1,32,128]{3,1,2,0:T(1,128)S(1)} %get-tuple-element.81), channel_id=1, source_target_pairs={{16,0},{32,16},{48,32},{64,48},{80,64},{96,80},{112,96},{128,112},... | collective-permute-start | bytes 196616 | tf_op jit(solution)/shard_map/ppermute | solution.py:18
  32.8 5.6 %collective-permute-start.6 = (f32[4,18,1,128]{3,1,2,0:T(8,128)S(1)}, f32[4,18,1,128]{3,1,2,0:T(8,128)S(1)}, u32[]{:S(2)}, u32[]{:S(2)}) collective-permute-start(f32[4,18,1,128]{3,1,2,0:T(8,128)S(1)} %get-tuple-element.78), channel_id=1, source_target_pairs={{0,1},{1,2},{2,3},{3,4},{4,5},{5,6},{6,7},{7,8},{8,9},{9,10},{10,1... | collective-permute-start | bytes 110600 | tf_op jit(solution)/shard_map/ppermute | solution.py:17
  34.7 6.7 %collective-permute-start.7 = (f32[4,18,1,128]{3,1,2,0:T(8,128)S(1)}, f32[4,18,1,128]{3,1,2,0:T(8,128)S(1)}, u32[]{:S(2)}, u32[]{:S(2)}) collective-permute-start(f32[4,18,1,128]{3,1,2,0:T(8,128)S(1)} %get-tuple-element.79), channel_id=1, source_target_pairs={{1,0},{2,1},{3,2},{4,3},{5,4},{6,5},{7,6},{8,7},{9,8},{10,9},{11,1... | collective-permute-start | bytes 110600 | tf_op jit(solution)/shard_map/ppermute | solution.py:18
  44.8 12.7 %collective-permute-start.8 = (f32[4,12,128]{2,0,1:T(4,128)S(1)}, f32[4,12,128]{2,0,1:T(4,128)S(1)}, u32[]{:S(2)}, u32[]{:S(2)}) collective-permute-start(f32[4,12,128]{2,0,1:T(4,128)S(1)} %pad_maximum_fusion.10), channel_id=1, source_target_pairs={{0,256},{256,0},{1,257},{257,1},{2,258},{258,2},{3,259},{259,3},{4... | collective-permute-start | bytes 73736 | tf_op jit(solution)/shard_map/ppermute | solution.py:30
where the time goes:
time: 120 us
  blocking collectives  60 us (50%)
  starting transfers between devices  32.4 us (27%)
  waiting for transfers between devices  14.5 us (12%)
  local copies, waits for them, and re-layouts  7.47 us (6%)
  other arithmetic  4.91 us (4%)
    all_gather x1, blocking collectives, local(): lax.all_gather(arrived[:, 0:row_share], 'colat', axis=1, tiled=True)  42.9 us
    all_gather x1, blocking collectives, local(): col_full = lax.all_gather(arrived[:, row_share:], 'lon', axis=1, tiled=True)  17.1 us
    ppermute x4, starting transfers between devices, with_halo(): before = lax.ppermute(last, axis, up)  13.4 us
    ppermute x1, starting transfers between devices, swapped(): return lax.ppermute(block, axis, route)  10.9 us
    ppermute x4, starting transfers between devices, with_halo(): after = lax.ppermute(leading, axis, down)  8.15 us
    ppermute x4, waiting for transfers between devices, with_halo(): after = lax.ppermute(leading, axis, down)  7.22 us
    ppermute x4, waiting for transfers between devices, with_halo(): before = lax.ppermute(last, axis, up)  5.49 us
    unnamed x22, local copies, waits for them, and re-layouts  2.63 us
  transfers between devices with their start and end apart: 9, of which 6 were waited for; matrix products, arithmetic and copies ran while one was open for 1% of the time, Pallas kernels for 0%

commit v1 on v0

--- a/solution.py
+++ b/solution.py
@@ -93,7 +93,12 @@
     turned_lon = sine_part * blended[2] + cosine * blended[3]
     blended = jnp.stack([blended[0], blended[1], turned_lat, turned_lon])
     arrived = swapped(blended, "panel", 0)
-    row_full = lax.all_gather(arrived[:, 0:row_share], "colat", axis=1, tiled=True)
+    row_full = jnp.concatenate(
+        lax.all_to_all(
+            jnp.stack([arrived[:, 0:row_share]] * lax.axis_size("colat")), "colat", 0, 0
+        ),
+        axis=1,
+    )
     col_full = lax.all_gather(arrived[:, row_share:], "lon", axis=1, tiled=True)
     col_blocks = col_full.reshape(4, 4, height, radial_len)
     west_strip = jnp.transpose(

time: 120 us -> 101 us (0.84)
  blocking collectives: 60 us -> 17.1 us
  starting transfers between devices: 32.4 us -> 45 us
  waiting for transfers between devices: 14.5 us -> 25.6 us
    all_gather x1 -> x0, blocking collectives: 42.9 us -> none  [local(): lax.all_gather(arrived[:, 0:row_share], 'colat', axis=1, tiled=True)]
    all_to_all x0 -> x1, starting transfers between devices: none -> 12.5 us  [local(): lax.all_to_all(jnp.stack([arrived[:, 0:row_share]] * lax.axis_size('colat...]
    all_to_all x0 -> x1, waiting for transfers between devices: none -> 11.1 us  [local(): lax.all_to_all(jnp.stack([arrived[:, 0:row_share]] * lax.axis_size('colat...]
    unnamed x22 -> x18, local copies, waits for them, and re-layouts: 2.63 us -> 2.35 us
  transfers between devices with their start and end apart: 9 -> 10, of which waited for: 6 -> 7; matrix products, arithmetic and copies ran while one was open for 1% -> 1% of each run, Pallas kernels for 0% -> 0%
where the time goes in v1:
time: 101 us
  starting transfers between devices  45 us (45%)
  waiting for transfers between devices  25.6 us (25%)
  blocking collectives  17.1 us (17%)
  local copies, waits for them, and re-layouts  7.95 us (8%)
  other arithmetic  4.89 us (5%)
    all_gather x1, blocking collectives, local(): col_full = lax.all_gather(arrived[:, row_share:], 'lon', axis=1, tiled=True)  17.1 us
    ppermute x4, starting transfers between devices, with_halo(): before = lax.ppermute(last, axis, up)  13.4 us
    all_to_all x1, starting transfers between devices, local(): lax.all_to_all(jnp.stack([arrived[:, 0:row_share]] * lax.axis_size('colat...  12.5 us
    all_to_all x1, waiting for transfers between devices, local(): lax.all_to_all(jnp.stack([arrived[:, 0:row_share]] * lax.axis_size('colat...  11.1 us
    ppermute x1, starting transfers between devices, swapped(): return lax.ppermute(block, axis, route)  10.9 us
    ppermute x4, starting transfers between devices, with_halo(): after = lax.ppermute(leading, axis, down)  8.15 us
    ppermute x4, waiting for transfers between devices, with_halo(): after = lax.ppermute(leading, axis, down)  7.22 us
    ppermute x4, waiting for transfers between devices, with_halo(): before = lax.ppermute(last, axis, up)  5.49 us
  transfers between devices with their start and end apart: 10, of which 7 were waited for; matrix products, arithmetic and copies ran while one was open for 1% of the time, Pallas kernels for 0%

profile of v1, /device:TPU:24, one launch (start us, length us, event | category | flops | bytes accessed | tf_op | source)
XLA Modules:
  0.0 101.0 jit_solution(13431827511904505346)
XLA Ops:
  0.0 0.0 copy-start
  0.0 1.9 %copy.68 = f32[4,1,16,32,128]{4,2,3,0,1:T(8,128)S(1)} copy(f32[4,1,16,32,128]{4,3,2,1,0:T(8,128)} %param.19) | data formatting | bytes 2097152 | tf_op args[0]
  1.9 0.0 copy-start.3
  1.9 0.1 fusion.16
  2.0 1.3 %collective-permute-start = (f32[4,2,32,128]{3,1,2,0:T(2,128)S(1)}, f32[4,2,32,128]{3,1,2,0:T(2,128)S(1)}, u32[]{:S(2)}, u32[]{:S(2)}) collective-permute-start(f32[4,2,32,128]{3,1,2,0:T(2,128)S(1)} %get-tuple-element.87), channel_id=1, source_target_pairs={{16,0},{32,16},{48,32},{64,48},{80,64},{96,80},{112,96},{128,112},... | collective-permute-start | bytes 393224 | tf_op jit(solution)/shard_map/ppermute | solution.py:18
  3.3 0.0 copy-start.1
  3.4 0.0 copy-start.2
  3.4 4.7 %collective-permute-start.1 = (f32[4,2,32,128]{3,1,2,0:T(2,128)S(1)}, f32[4,2,32,128]{3,1,2,0:T(2,128)S(1)}, u32[]{:S(2)}, u32[]{:S(2)}) collective-permute-start(f32[4,2,32,128]{3,1,2,0:T(2,128)S(1)} %get-tuple-element.86), channel_id=1, source_target_pairs={{0,16},{16,32},{32,48},{48,64},{64,80},{80,96},{96,112},{112,128},... | collective-permute-start | bytes 393224 | tf_op jit(solution)/shard_map/ppermute | solution.py:17
  8.1 0.0 copy-done
  8.1 0.1 fusion.15
  8.2 0.0 copy-done.3
  8.2 0.0 copy-start.4
  8.2 0.0 copy-start.5
  8.2 0.0 copy-start.6
  8.3 0.2 copy.44
  8.4 0.2 copy.45
  8.6 0.2 copy.46
  8.8 0.0 copy-done.1
  8.8 0.2 copy.40
  8.9 0.0 copy-done.2
  9.0 0.2 copy.41
  9.1 0.0 copy-done.4
  9.1 0.0 copy-done.5
  9.2 0.0 copy-done.6
  9.2 0.0 collective-permute-done
  9.2 1.3 %collective-permute-done.1 = f32[4,2,32,128]{3,1,2,0:T(2,128)S(1)} collective-permute-done((f32[4,2,32,128]{3,1,2,0:T(2,128)S(1)}, f32[4,2,32,128]{3,1,2,0:T(2,128)S(1)}, u32[]{:S(2)}, u32[]{:S(2)}) %collective-permute-start.1) | collective-permute-done | bytes 131104 | tf_op jit(solution)/shard_map/ppermute | solution.py:17
  10.6 1.9 %collective-permute-start.2 = (f32[4,20,2,128]{3,1,2,0:T(8,128)S(1)}, f32[4,20,2,128]{3,1,2,0:T(8,128)S(1)}, u32[]{:S(2)}, u32[]{:S(2)}) collective-permute-start(f32[4,20,2,128]{3,1,2,0:T(8,128)S(1)} %get-tuple-element.76), channel_id=1, source_target_pairs={{1,0},{2,1},{3,2},{4,3},{5,4},{6,5},{7,6},{8,7},{9,8},{10,9},{11,1... | collective-permute-start | bytes 245768 | tf_op jit(solution)/shard_map/ppermute | solution.py:18
  12.5 2.4 %collective-permute-start.3 = (f32[4,20,2,128]{3,1,2,0:T(8,128)S(1)}, f32[4,20,2,128]{3,1,2,0:T(8,128)S(1)}, u32[]{:S(2)}, u32[]{:S(2)}) collective-permute-start(f32[4,20,2,128]{3,1,2,0:T(8,128)S(1)} %get-tuple-element.77), channel_id=1, source_target_pairs={{0,1},{1,2},{2,3},{3,4},{4,5},{5,6},{6,7},{7,8},{8,9},{9,10},{10,1... | collective-permute-start | bytes 245768 | tf_op jit(solution)/shard_map/ppermute | solution.py:17
  14.9 0.0 collective-permute-done.2
  15.0 3.5 %collective-permute-done.3 = f32[4,20,2,128]{3,1,2,0:T(8,128)S(1)} collective-permute-done((f32[4,20,2,128]{3,1,2,0:T(8,128)S(1)}, f32[4,20,2,128]{3,1,2,0:T(8,128)S(1)}, u32[]{:S(2)}, u32[]{:S(2)}) %collective-permute-start.3) | collective-permute-done | bytes 81952 | tf_op jit(solution)/shard_map/ppermute | solution.py:17
  18.5 0.3 pad_maximum_fusion
  18.7 2.5 %fusion.2 = f32[4,16,32,128]{3,1,2,0:T(8,128)S(1)} fusion(f32[1,16,32,128]{3,1,2,0:T(8,128)S(1)} %copy.41, f32[1,16,32,128]{3,1,2,0:T(8,128)S(1)} %copy.40, f32[4,20,34,128]{3,1,2,0:T(8,128)S(1)} %get-tuple-element.75, f32[4,20,34,128]{3,1,2,0:T(8,128)S(1)} %get-tuple-element.74, f32[4,2,32,128]{3,1,2,0:T(2,128)S(1)} %collective-permute-done, ...), kind=kLoop, calls=%fused_computation.20 | loop fusion | flops 11796480 | bytes 7864320 | tf_op jit(solution)/shard_map/sub | solution.py:57
  21.2 0.2 fusion.3
  21.5 0.7 multiply_add_fusion
  22.1 0.1 fusion.14
  22.2 4.4 %collective-permute-start.4 = (f32[4,1,32,128]{3,1,2,0:T(1,128)S(1)}, f32[4,1,32,128]{3,1,2,0:T(1,128)S(1)}, u32[]{:S(2)}, u32[]{:S(2)}) collective-permute-start(f32[4,1,32,128]{3,1,2,0:T(1,128)S(1)} %get-tuple-element.80), channel_id=1, source_target_pairs={{0,16},{16,32},{32,48},{48,64},{64,80},{80,96},{96,112},{112,128},... | collective-permute-start | bytes 196616 | tf_op jit(solution)/shard_map/ppermute | solution.py:17
  26.6 1.3 %collective-permute-start.5 = (f32[4,1,32,128]{3,1,2,0:T(1,128)S(1)}, f32[4,1,32,128]{3,1,2,0:T(1,128)S(1)}, u32[]{:S(2)}, u32[]{:S(2)}) collective-permute-start(f32[4,1,32,128]{3,1,2,0:T(1,128)S(1)} %get-tuple-element.81), channel_id=1, source_target_pairs={{16,0},{32,16},{48,32},{64,48},{80,64},{96,80},{112,96},{128,112},... | collective-permute-start | bytes 196616 | tf_op jit(solution)/shard_map/ppermute | solution.py:18
  27.9 0.7 collective-permute-done.4
  28.6 4.2 %collective-permute-done.5 = f32[4,1,32,128]{3,1,2,0:T(1,128)S(1)} collective-permute-done((f32[4,1,32,128]{3,1,2,0:T(1,128)S(1)}, f32[4,1,32,128]{3,1,2,0:T(1,128)S(1)}, u32[]{:S(2)}, u32[]{:S(2)}) %collective-permute-start.5) | collective-permute-done | bytes 65568 | tf_op jit(solution)/shard_map/ppermute | solution.py:18
  32.8 1.9 %collective-permute-start.6 = (f32[4,18,1,128]{3,1,2,0:T(8,128)S(1)}, f32[4,18,1,128]{3,1,2,0:T(8,128)S(1)}, u32[]{:S(2)}, u32[]{:S(2)}) collective-permute-start(f32[4,18,1,128]{3,1,2,0:T(8,128)S(1)} %get-tuple-element.78), channel_id=1, source_target_pairs={{0,1},{1,2},{2,3},{3,4},{4,5},{5,6},{6,7},{7,8},{8,9},{9,10},{10,1... | collective-permute-start | bytes 110600 | tf_op jit(solution)/shard_map/ppermute | solution.py:17
  34.7 3.6 %collective-permute-start.7 = (f32[4,18,1,128]{3,1,2,0:T(8,128)S(1)}, f32[4,18,1,128]{3,1,2,0:T(8,128)S(1)}, u32[]{:S(2)}, u32[]{:S(2)}) collective-permute-start(f32[4,18,1,128]{3,1,2,0:T(8,128)S(1)} %get-tuple-element.79), channel_id=1, source_target_pairs={{1,0},{2,1},{3,2},{4,3},{5,4},{6,5},{7,6},{8,7},{9,8},{10,9},{11,1... | collective-permute-start | bytes 110600 | tf_op jit(solution)/shard_map/ppermute | solution.py:18
  38.4 0.0 collective-permute-done.6
  38.4 3.1 %collective-permute-done.7 = f32[4,18,1,128]{3,1,2,0:T(8,128)S(1)} collective-permute-done((f32[4,18,1,128]{3,1,2,0:T(8,128)S(1)}, f32[4,18,1,128]{3,1,2,0:T(8,128)S(1)}, u32[]{:S(2)}, u32[]{:S(2)}) %collective-permute-start.7) | collective-permute-done | bytes 36896 | tf_op jit(solution)/shard_map/ppermute | solution.py:18
  41.4 0.3 pad_maximum_fusion.1
  41.7 0.5 copy.48
  42.2 0.6 gather_fusion.2
  42.8 0.6 gather_fusion.3
  43.4 0.6 gather_fusion.1
  43.9 0.6 gather_fusion
  44.5 0.2 fusion.11
  44.7 0.1 multiply_subtract_fusion
  44.8 10.9 %collective-permute-start.8 = (f32[4,12,128]{2,0,1:T(4,128)S(1)}, f32[4,12,128]{2,0,1:T(4,128)S(1)}, u32[]{:S(2)}, u32[]{:S(2)}) collective-permute-start(f32[4,12,128]{2,0,1:T(4,128)S(1)} %pad_maximum_fusion.10), channel_id=1, source_target_pairs={{0,256},{256,0},{1,257},{257,1},{2,258},{258,2},{3,259},{259,3},{4... | collective-permute-start | bytes 73736 | tf_op jit(solution)/shard_map/ppermute | solution.py:30
  55.8 1.8 %collective-permute-done.8 = f32[4,12,128]{2,0,1:T(4,128)S(1)} collective-permute-done((f32[4,12,128]{2,0,1:T(4,128)S(1)}, f32[4,12,128]{2,0,1:T(4,128)S(1)}, u32[]{:S(2)}, u32[]{:S(2)}) %collective-permute-start.8) | collective-permute-done | bytes 24608 | tf_op jit(solution)/shard_map/ppermute | solution.py:30
  57.6 17.1 %all_gather.3 = f32[4,64,128]{2,0,1:T(4,128)S(1)} all-gather(f32[4,4,128]{2,0,1:T(4,128)S(1)} %slice.349), channel_id=1, replica_groups=mesh['panel'=2,'colat'=16,'lon'=16] {'lon'}, dimensions={1}, use_global_device_ids=true | all-gather | bytes 139264 | tf_op jit(solution)/shard_map/all_gather | solution.py:102
  74.7 0.7 stack.19
  75.4 12.5 %all-to-all-start = ((f32[16,4,8,128]{3,2,1,0:T(8,128)}), f32[16,4,8,128]{3,2,1,0:T(8,128)S(1)}, u32[]{:S(2)}, u32[]{:S(2)}) async-start(f32[16,4,8,128]{3,2,1,0:T(8,128)} %stack.19), calls=%async_computation | async-start | bytes 524288 | tf_op jit(solution)/shard_map/all_to_all | solution.py:97
  88.0 11.1 %all-to-all-done = f32[16,4,8,128]{3,2,1,0:T(8,128)S(1)} async-done(((f32[16,4,8,128]{3,2,1,0:T(8,128)}), f32[16,4,8,128]{3,2,1,0:T(8,128)S(1)}, u32[]{:S(2)}, u32[]{:S(2)}) %all-to-all-start) | async-done | bytes 262176 | tf_op jit(solution)/shard_map/all_to_all | solution.py:97
  99.2 0.2 fusion.6
  99.4 0.1 copy.73
  99.5 0.2 fusion.5
  99.7 1.3 %copy.56 = f32[4,1,16,32,128]{4,3,2,1,0:T(8,128)} copy(f32[4,1,16,32,128]{4,2,3,0,1:T(8,128)S(1)} %fusion.5) | data formatting | bytes 2097152 | tf_op jit(solution)/shard_map/scatter | solution.py:118
  (22 shorter events, 0.3 us)
Async XLA Ops:
  0.0 8.1 %copy-start = (f32[4,1,16,32,128]{4,3,2,1,0:T(8,128)S(1)}, f32[4,1,16,32,128]{4,3,2,1,0:T(8,128)}, u32[]{:S(2)}) copy-start(f32[4,1,16,32,128]{4,3,2,1,0:T(8,128)} %param.19) | copy-start | bytes 3145732
  1.9 6.3 %copy-start.3 = (f32[1,1,1,2,12]{4,3,2,1,0:T(2,128)S(1)}, f32[1,1,1,2,12]{4,3,2,1,0:T(2,128)}, u32[]{:S(2)}) copy-start(f32[1,1,1,2,12]{4,3,2,1,0:T(2,128)} %param.24) | copy-start | bytes 292
  2.0 7.2 %collective-permute-start = (f32[4,2,32,128]{3,1,2,0:T(2,128)S(1)}, f32[4,2,32,128]{3,1,2,0:T(2,128)S(1)}, u32[]{:S(2)}, u32[]{:S(2)}) collective-permute-start(f32[4,2,32,128]{3,1,2,0:T(2,128)S(1)} %get-tuple-element.87), channel_id=1, source_target_pairs={{16,0},{32,16},{48,32},{64,48},{80,64},{96,80},{112,96},{128,112},... | collective-permute-start | bytes 393224 | tf_op jit(solution)/shard_map/ppermute | solution.py:18
  3.3 5.4 %copy-start.1 = (f32[1,16,32,128]{3,2,1,0:T(8,128)S(1)}, f32[1,16,32,128]{3,2,1,0:T(8,128)}, u32[]{:S(2)}) copy-start(f32[1,16,32,128]{3,2,1,0:T(8,128)} %param.20) | copy-start | bytes 786436
  3.4 5.6 %copy-start.2 = (f32[1,16,32,128]{3,2,1,0:T(8,128)S(1)}, f32[1,16,32,128]{3,2,1,0:T(8,128)}, u32[]{:S(2)}) copy-start(f32[1,16,32,128]{3,2,1,0:T(8,128)} %param.21) | copy-start | bytes 786436
  3.4 7.2 %collective-permute-start.1 = (f32[4,2,32,128]{3,1,2,0:T(2,128)S(1)}, f32[4,2,32,128]{3,1,2,0:T(2,128)S(1)}, u32[]{:S(2)}, u32[]{:S(2)}) collective-permute-start(f32[4,2,32,128]{3,1,2,0:T(2,128)S(1)} %get-tuple-element.86), channel_id=1, source_target_pairs={{0,16},{16,32},{32,48},{48,64},{64,80},{80,96},{96,112},{112,128},... | collective-permute-start | bytes 393224 | tf_op jit(solution)/shard_map/ppermute | solution.py:17
  8.2 0.9 copy-start.4
  8.2 0.9 copy-start.5
  8.2 0.9 copy-start.6
  10.6 4.4 %collective-permute-start.2 = (f32[4,20,2,128]{3,1,2,0:T(8,128)S(1)}, f32[4,20,2,128]{3,1,2,0:T(8,128)S(1)}, u32[]{:S(2)}, u32[]{:S(2)}) collective-permute-start(f32[4,20,2,128]{3,1,2,0:T(8,128)S(1)} %get-tuple-element.76), channel_id=1, source_target_pairs={{1,0},{2,1},{3,2},{4,3},{5,4},{6,5},{7,6},{8,7},{9,8},{10,9},{11,1... | collective-permute-start | bytes 245768 | tf_op jit(solution)/shard_map/ppermute | solution.py:18
  12.5 5.9 %collective-permute-start.3 = (f32[4,20,2,128]{3,1,2,0:T(8,128)S(1)}, f32[4,20,2,128]{3,1,2,0:T(8,128)S(1)}, u32[]{:S(2)}, u32[]{:S(2)}) collective-permute-start(f32[4,20,2,128]{3,1,2,0:T(8,128)S(1)} %get-tuple-element.77), channel_id=1, source_target_pairs={{0,1},{1,2},{2,3},{3,4},{4,5},{5,6},{6,7},{7,8},{8,9},{9,10},{10,1... | collective-permute-start | bytes 245768 | tf_op jit(solution)/shard_map/ppermute | solution.py:17
  22.2 6.4 %collective-permute-start.4 = (f32[4,1,32,128]{3,1,2,0:T(1,128)S(1)}, f32[4,1,32,128]{3,1,2,0:T(1,128)S(1)}, u32[]{:S(2)}, u32[]{:S(2)}) collective-permute-start(f32[4,1,32,128]{3,1,2,0:T(1,128)S(1)} %get-tuple-element.80), channel_id=1, source_target_pairs={{0,16},{16,32},{32,48},{48,64},{64,80},{80,96},{96,112},{112,128},... | collective-permute-start | bytes 196616 | tf_op jit(solution)/shard_map/ppermute | solution.py:17
  26.6 6.2 %collective-permute-start.5 = (f32[4,1,32,128]{3,1,2,0:T(1,128)S(1)}, f32[4,1,32,128]{3,1,2,0:T(1,128)S(1)}, u32[]{:S(2)}, u32[]{:S(2)}) collective-permute-start(f32[4,1,32,128]{3,1,2,0:T(1,128)S(1)} %get-tuple-element.81), channel_id=1, source_target_pairs={{16,0},{32,16},{48,32},{64,48},{80,64},{96,80},{112,96},{128,112},... | collective-permute-start | bytes 196616 | tf_op jit(solution)/shard_map/ppermute | solution.py:18
  32.8 5.6 %collective-permute-start.6 = (f32[4,18,1,128]{3,1,2,0:T(8,128)S(1)}, f32[4,18,1,128]{3,1,2,0:T(8,128)S(1)}, u32[]{:S(2)}, u32[]{:S(2)}) collective-permute-start(f32[4,18,1,128]{3,1,2,0:T(8,128)S(1)} %get-tuple-element.78), channel_id=1, source_target_pairs={{0,1},{1,2},{2,3},{3,4},{4,5},{5,6},{6,7},{7,8},{8,9},{9,10},{10,1... | collective-permute-start | bytes 110600 | tf_op jit(solution)/shard_map/ppermute | solution.py:17
  34.7 6.7 %collective-permute-start.7 = (f32[4,18,1,128]{3,1,2,0:T(8,128)S(1)}, f32[4,18,1,128]{3,1,2,0:T(8,128)S(1)}, u32[]{:S(2)}, u32[]{:S(2)}) collective-permute-start(f32[4,18,1,128]{3,1,2,0:T(8,128)S(1)} %get-tuple-element.79), channel_id=1, source_target_pairs={{1,0},{2,1},{3,2},{4,3},{5,4},{6,5},{7,6},{8,7},{9,8},{10,9},{11,1... | collective-permute-start | bytes 110600 | tf_op jit(solution)/shard_map/ppermute | solution.py:18
  44.8 12.7 %collective-permute-start.8 = (f32[4,12,128]{2,0,1:T(4,128)S(1)}, f32[4,12,128]{2,0,1:T(4,128)S(1)}, u32[]{:S(2)}, u32[]{:S(2)}) collective-permute-start(f32[4,12,128]{2,0,1:T(4,128)S(1)} %pad_maximum_fusion.10), channel_id=1, source_target_pairs={{0,256},{256,0},{1,257},{257,1},{2,258},{258,2},{3,259},{259,3},{4... | collective-permute-start | bytes 73736 | tf_op jit(solution)/shard_map/ppermute | solution.py:30
  75.4 23.7 %all-to-all-start = ((f32[16,4,8,128]{3,2,1,0:T(8,128)}), f32[16,4,8,128]{3,2,1,0:T(8,128)S(1)}, u32[]{:S(2)}, u32[]{:S(2)}) async-start(f32[16,4,8,128]{3,2,1,0:T(8,128)} %stack.19), calls=%async_computation | async-start | bytes 524288 | tf_op jit(solution)/shard_map/all_to_all | solution.py:97
